TPU v7x, 32 devices: a whole 2x2x4 slice. The times are simulated.
32 devices in a mesh: dp: 16 (over z, x, core), tensor: 2 (over y).
Axes of the slice: x: 2, y: 2, z: 4, core: 2. Of those that a mesh axis runs over, the one named last changes fastest.
Arguments:
- layer_input: bfloat16 [2, 8192, 1024], P(None, ('dp', 'tensor')), may hold values from -6 to 6
- segment_ids: int32 [2, 8192], P(None, 'dp'), may hold values from 0 to 5, as said below
- qkv_weight: bfloat16 [3, 1024, 1024], P(None, 'dp', 'tensor'), may hold values from -0.1875 to 0.1875
- qv_bias: bfloat16 [2, 16, 64], P(None, 'tensor', 'dp'), may hold values from -3 to 3
- out_weight: bfloat16 [1024, 1024], P('tensor', 'dp'), may hold values from -1 to 1
- up_weight: bfloat16 [1024, 4096], P('dp', 'tensor'), may hold values from -0.1875 to 0.1875
- up_bias: bfloat16 [2, 2048], P('tensor', 'dp'), may hold values from -3 to 3
- down_weight: bfloat16 [4096, 1024], P('tensor', 'dp'), may hold values from -0.09375 to 0.09375
- norm_gains: float32 [2, 1024], P(None, ('dp', 'tensor')), may hold values from 0.1 to 1.9
- row_biases: float32 [4, 1024], P(None, ('dp', 'tensor')), may hold values from -2 to 2
- cotangent: bfloat16 [2, 8192, 1024], P(None, ('dp', 'tensor')), may hold values from -6 to 6
Outputs:
- layer_output: bfloat16 [2, 8192, 1024], P(None, ('dp', 'tensor'))
- input_grad: bfloat16 [2, 8192, 1024], P(None, ('dp', 'tensor'))
- qkv_weight_grad: float32 [3, 1024, 1024], P(None, 'dp', 'tensor')
- qv_bias_grad: float32 [2, 16, 64], P(None, 'tensor', 'dp')
- out_weight_grad: float32 [1024, 1024], P('tensor', 'dp')
- up_weight_grad: float32 [1024, 4096], P('dp', 'tensor')
- up_bias_grad: float32 [2, 2048], P('tensor', 'dp')
- down_weight_grad: float32 [4096, 1024], P('tensor', 'dp')
- norm_gains_grad: float32 [2, 1024], P(None, ('dp', 'tensor'))
- row_biases_grad: float32 [4, 1024], P(None, ('dp', 'tensor'))
Inputs may be any that keep to these rules, and one draw needn't show every extreme that they name: `segment_ids`: within every sequence of 512 rows, documents 1 to 5 follow one another in order, each 20 to 100 tokens long, and padding with id 0 fills the rest, 12 tokens or more.
All inputs are finite; a program needn't handle non-finite values.
Results may differ from a plain program's by a relative error of at most 0.02.
Values may be sent and summed in bfloat16 or wider, within the bound.
No kernel may reach another device: no remote copies, remote signals or barrier semaphores. Data moves between devices by JAX's collectives and lax.ppermute only.
A program may use at most 192 MiB of HBM per device.

v0:
```python
import jax
import jax.numpy as jnp
from jax import lax
from jax.sharding import PartitionSpec as P

HEAD_DIM = 64


def gelu_exact(values):
    return jax.nn.gelu(values, approximate=False)


def normalize(rows, gain, shift):
    centered = rows - jnp.mean(rows, axis=-1, keepdims=True)
    variance = jnp.mean(centered * centered, axis=-1, keepdims=True)
    inverse = lax.rsqrt(variance + 1e-05)
    normed = centered * inverse
    return (normed * gain + shift, normed, inverse)


def norm_back(grad, normed, inverse, gain):
    scaled = grad * gain
    return inverse * (
        scaled
        - jnp.mean(scaled, axis=-1, keepdims=True)
        - normed * jnp.mean(scaled * normed, axis=-1, keepdims=True)
    )


def attend(query, keys, values, keep_mask, scale):
    scores = jnp.einsum("qhd,khd->hqk", query, keys, preferred_element_type=jnp.float32) * scale
    masked = jnp.where(keep_mask[None], scores, -1e30)
    highest = jnp.max(masked, axis=-1, keepdims=True)
    shifted = jnp.exp(masked - highest)
    totals = jnp.sum(shifted, axis=-1, keepdims=True)
    probs = (shifted / totals).astype(jnp.bfloat16)
    context = jnp.einsum("hqk,khd->qhd", probs, values, preferred_element_type=jnp.float32)
    return (context, highest + jnp.log(totals))


def attend_back(query, keys, values, keep_mask, logsumexp, grad_context, scale):
    scores = jnp.einsum("qhd,khd->hqk", query, keys, preferred_element_type=jnp.float32) * scale
    masked = jnp.where(keep_mask[None], scores, -1e30)
    probs = jnp.exp(masked - logsumexp)
    probs_low = probs.astype(jnp.bfloat16)
    grad_values = jnp.einsum(
        "hqk,qhd->khd", probs_low, grad_context, preferred_element_type=jnp.float32
    )
    grad_probs = jnp.einsum(
        "qhd,khd->hqk", grad_context, values, preferred_element_type=jnp.float32
    )
    grad_scores = probs * (grad_probs - jnp.sum(probs * grad_probs, axis=-1, keepdims=True))
    grad_low = grad_scores.astype(jnp.bfloat16)
    grad_query = (
        jnp.einsum("hqk,khd->qhd", grad_low, keys, preferred_element_type=jnp.float32) * scale
    )
    grad_keys = (
        jnp.einsum("hqk,qhd->khd", grad_low, query, preferred_element_type=jnp.float32) * scale
    )
    return (grad_query, grad_keys, grad_values)


def local(
    layer_input,
    segment_ids,
    qkv_weight,
    qv_bias,
    out_weight,
    up_weight,
    up_bias,
    down_weight,
    norm_gains,
    row_biases,
    cotangent,
):
    gains_all, biases_all = (
        lax.all_gather(norm_gains, ("dp", "tensor"), axis=1, tiled=True),
        lax.all_gather(row_biases, ("dp", "tensor"), axis=1, tiled=True),
    )
    shards = (qkv_weight, qv_bias, out_weight, up_weight, up_bias, down_weight)
    dp_count = lax.axis_size("dp")
    seq_len = segment_ids.shape[1]
    heads_local = qv_bias.shape[1]
    width_local = heads_local * HEAD_DIM
    scale = HEAD_DIM ** (-0.5)

    def micro_step(carry, inputs):
        rows_in, segments, grad_rows = inputs
        qkv_full, qv_full, out_full, up_full, upb_full, down_full = (
            lax.all_gather(shards[0], "dp", axis=1, tiled=True),
            lax.all_gather(shards[1], "dp", axis=2, tiled=True),
            lax.all_gather(shards[2], "dp", axis=1, tiled=True),
            lax.all_gather(shards[3], "dp", axis=0, tiled=True),
            lax.all_gather(shards[4], "dp", axis=1, tiled=True),
            lax.all_gather(shards[5], "dp", axis=1, tiled=True),
        )
        gathered = lax.all_gather(rows_in, "tensor", axis=0, tiled=True)
        projected = jnp.einsum(
            "rd,kdc->krc", gathered, qkv_full, preferred_element_type=jnp.float32
        )
        bias_flat = qv_full.reshape(2, width_local).astype(jnp.float32)
        split = (seq_len, heads_local, HEAD_DIM)
        query = (projected[0] + bias_flat[0]).astype(jnp.bfloat16).reshape(split)
        keys = projected[1].astype(jnp.bfloat16).reshape(split)
        values = (projected[2] + bias_flat[1]).astype(jnp.bfloat16).reshape(split)
        keep_mask = segments[:, None] == segments[None, :]
        attended, logsumexp = attend(query, keys, values, keep_mask, scale)
        context = attended.reshape(seq_len, width_local).astype(jnp.bfloat16)
        attention = lax.psum_scatter(
            jnp.dot(context, out_full, preferred_element_type=jnp.float32).astype(jnp.bfloat16),
            "tensor",
            scatter_dimension=0,
            tiled=True,
        ).astype(jnp.float32)
        residual_one = rows_in.astype(jnp.float32) + attention + biases_all[0]
        hidden, normed_one, inverse_one = normalize(residual_one, gains_all[0], biases_all[1])
        hidden_rows = lax.all_gather(hidden.astype(jnp.bfloat16), "tensor", axis=0, tiled=True)
        upper = jnp.dot(
            hidden_rows, up_full, preferred_element_type=jnp.float32
        ) + upb_full.reshape(-1).astype(jnp.float32)
        activated = gelu_exact(upper).astype(jnp.bfloat16)
        branch = lax.psum_scatter(
            jnp.dot(activated, down_full, preferred_element_type=jnp.float32).astype(jnp.bfloat16),
            "tensor",
            scatter_dimension=0,
            tiled=True,
        ).astype(jnp.float32)
        residual_two = hidden + branch + biases_all[2]
        result, normed_two, inverse_two = normalize(residual_two, gains_all[1], biases_all[3])
        qkv_back, qv_back, out_back, up_back, upb_back, down_back = (
            lax.all_gather(shards[0], "dp", axis=1, tiled=True),
            lax.all_gather(shards[1], "dp", axis=2, tiled=True),
            lax.all_gather(shards[2], "dp", axis=1, tiled=True),
            lax.all_gather(shards[3], "dp", axis=0, tiled=True),
            lax.all_gather(shards[4], "dp", axis=1, tiled=True),
            lax.all_gather(shards[5], "dp", axis=1, tiled=True),
        )
        grad_output = grad_rows.astype(jnp.float32)
        gain_two_grad = jnp.sum(grad_output * normed_two, axis=0)
        shift_two_grad = jnp.sum(grad_output, axis=0)
        grad_two = norm_back(grad_output, normed_two, inverse_two, gains_all[1])
        down_bias_grad = jnp.sum(grad_two, axis=0)
        branch_rows = lax.all_gather(grad_two.astype(jnp.bfloat16), "tensor", axis=0, tiled=True)
        down_grad = jnp.einsum(
            "rf,rd->fd", activated, branch_rows, preferred_element_type=jnp.float32
        )
        grad_active = jnp.einsum(
            "rd,fd->rf", branch_rows, down_back, preferred_element_type=jnp.float32
        )
        gelu_pull = jax.vjp(gelu_exact, upper)[1]
        grad_upper = gelu_pull(grad_active)[0].astype(jnp.bfloat16)
        up_bias_grad = jnp.sum(grad_upper.astype(jnp.float32), axis=0).reshape(1, -1)
        up_grad = jnp.einsum(
            "rd,rf->df", hidden_rows, grad_upper, preferred_element_type=jnp.float32
        )
        grad_hidden = grad_two + lax.psum_scatter(
            jnp.einsum("rf,df->rd", grad_upper, up_back, preferred_element_type=jnp.float32).astype(
                jnp.bfloat16
            ),
            "tensor",
            scatter_dimension=0,
            tiled=True,
        ).astype(jnp.float32)
        gain_one_grad = jnp.sum(grad_hidden * normed_one, axis=0)
        shift_one_grad = jnp.sum(grad_hidden, axis=0)
        grad_one = norm_back(grad_hidden, normed_one, inverse_one, gains_all[0])
        out_bias_grad = jnp.sum(grad_one, axis=0)
        attention_rows = lax.all_gather(grad_one.astype(jnp.bfloat16), "tensor", axis=0, tiled=True)
        out_grad = jnp.einsum(
            "rc,rd->cd", context, attention_rows, preferred_element_type=jnp.float32
        )
        grad_context = (
            jnp.einsum("rd,cd->rc", attention_rows, out_back, preferred_element_type=jnp.float32)
            .astype(jnp.bfloat16)
            .reshape(split)
        )
        grad_query, grad_keys, grad_values = attend_back(
            query, keys, values, keep_mask, logsumexp, grad_context, scale
        )
        grad_qkv = (
            jnp.stack([grad_query, grad_keys, grad_values])
            .reshape(3, seq_len, width_local)
            .astype(jnp.bfloat16)
        )
        bias_sums = jnp.sum(jnp.stack([grad_qkv[0], grad_qkv[2]]).astype(jnp.float32), axis=1)
        qv_grad = bias_sums.reshape(2, heads_local, HEAD_DIM)
        qkv_grad = jnp.einsum("rd,krc->kdc", gathered, grad_qkv, preferred_element_type=jnp.float32)
        input_grad = (
            grad_one
            + lax.psum_scatter(
                jnp.einsum(
                    "krc,kdc->rd", grad_qkv, qkv_back, preferred_element_type=jnp.float32
                ).astype(jnp.bfloat16),
                "tensor",
                scatter_dimension=0,
                tiled=True,
            ).astype(jnp.float32)
        ).astype(jnp.bfloat16)
        gains_grad = jnp.stack([gain_one_grad, gain_two_grad])
        biases_grad = jnp.stack([out_bias_grad, shift_one_grad, down_bias_grad, shift_two_grad])
        updates = (
            qkv_grad,
            qv_grad,
            out_grad,
            up_grad,
            up_bias_grad,
            down_grad,
            gains_grad,
            biases_grad,
        )
        carry = tuple((total + update for total, update in zip(carry, updates)))
        return (carry, (result.astype(jnp.bfloat16), input_grad))

    initial = (
        jnp.zeros((3, qkv_weight.shape[1] * dp_count, qkv_weight.shape[2]), jnp.float32),
        jnp.zeros((2, qv_bias.shape[1], qv_bias.shape[2] * dp_count), jnp.float32),
        jnp.zeros((out_weight.shape[0], out_weight.shape[1] * dp_count), jnp.float32),
        jnp.zeros((up_weight.shape[0] * dp_count, up_weight.shape[1]), jnp.float32),
        jnp.zeros((1, up_bias.shape[1] * dp_count), jnp.float32),
        jnp.zeros((down_weight.shape[0], down_weight.shape[1] * dp_count), jnp.float32),
        jnp.zeros(gains_all.shape, jnp.float32),
        jnp.zeros(biases_all.shape, jnp.float32),
    )
    totals, (outputs, input_grads) = lax.scan(
        micro_step, initial, (layer_input, segment_ids, cotangent)
    )
    qkv_sum, qv_sum, out_sum, up_sum, upb_sum, down_sum = (
        lax.psum_scatter(
            totals[0].astype(jnp.bfloat16), "dp", scatter_dimension=1, tiled=True
        ).astype(jnp.float32),
        lax.psum_scatter(
            totals[1].astype(jnp.bfloat16), "dp", scatter_dimension=2, tiled=True
        ).astype(jnp.float32),
        lax.psum_scatter(
            totals[2].astype(jnp.bfloat16), "dp", scatter_dimension=1, tiled=True
        ).astype(jnp.float32),
        lax.psum_scatter(
            totals[3].astype(jnp.bfloat16), "dp", scatter_dimension=0, tiled=True
        ).astype(jnp.float32),
        lax.psum_scatter(
            totals[4].astype(jnp.bfloat16), "dp", scatter_dimension=1, tiled=True
        ).astype(jnp.float32),
        lax.psum_scatter(
            totals[5].astype(jnp.bfloat16), "dp", scatter_dimension=1, tiled=True
        ).astype(jnp.float32),
    )
    gains_sum, biases_sum = (
        lax.psum_scatter(totals[6], ("dp", "tensor"), scatter_dimension=1, tiled=True),
        lax.psum_scatter(totals[7], ("dp", "tensor"), scatter_dimension=1, tiled=True),
    )
    return (
        outputs,
        input_grads,
        qkv_sum,
        qv_sum,
        out_sum,
        up_sum,
        upb_sum,
        down_sum,
        gains_sum,
        biases_sum,
    )


def solution(mesh):
    return jax.shard_map(
        local,
        mesh=mesh,
        in_specs=(
            P(None, ("dp", "tensor"), None),
            P(None, "dp"),
            P(None, "dp", "tensor"),
            P(None, "tensor", "dp"),
            P("tensor", "dp"),
            P("dp", "tensor"),
            P("tensor", "dp"),
            P("tensor", "dp"),
            P(None, ("dp", "tensor")),
            P(None, ("dp", "tensor")),
            P(None, ("dp", "tensor"), None),
        ),
        out_specs=(
            P(None, ("dp", "tensor"), None),
            P(None, ("dp", "tensor"), None),
            P(None, "dp", "tensor"),
            P(None, "tensor", "dp"),
            P("tensor", "dp"),
            P("dp", "tensor"),
            P("tensor", "dp"),
            P("tensor", "dp"),
            P(None, ("dp", "tensor")),
            P(None, ("dp", "tensor")),
        ),
        check_vma=False,
    )
```

profile of v0, /device:TPU:0, one launch (start us, length us, event | category | flops | bytes accessed | tf_op | source)
XLA Modules:
  0.0 1591.5 jit_solution(6932965279047940089)
XLA Ops:
  8.8 70.0 %all-gather.2 = f32[32,32,2]{1,2,0:T(2,128)S(1)} all-gather(f32[1,32,2]{1,2,0:T(2,128)} %bitcast.322), channel_id=1, replica_groups=mesh['dp'=16,'tensor'=2] {'dp','tensor'}, dimensions={0}, use_global_device_ids=true | all-gather | bytes 8448 | tf_op jit(solution)/shard_map/all_gather | solution.py:77
  78.8 63.9 %all-gather.1 = f32[32,32,4]{1,2,0:T(4,128)S(1)} all-gather(f32[1,32,4]{1,2,0:T(4,128)} %bitcast.321), channel_id=1, replica_groups=mesh['dp'=16,'tensor'=2] {'dp','tensor'}, dimensions={0}, use_global_device_ids=true | all-gather | bytes 16896 | tf_op jit(solution)/shard_map/all_gather | solution.py:78
  142.9 834.0 %while.29 = (s32[]{:T(128)}, f32[3,1024,512]{1,2,0:T(8,128)}, f32[2,8,64]{2,1,0:T(8,128)S(1)}, f32[512,1024]{1,0:T(8,128)}, f32[1024,2048]{1,0:T(8,128)}, /*inde...) while((s32[]{:T(128)}, f32[3,1024,512]{1,2,0:T(8,128)}, ...), condition=%wide.region_24.25_spmd.clone, body=%wide.region_0.24_spmd.clone.sunk | while | flops 21109161984 | bytes 468527744 | solution.py:224
  147.4 17.2 %all_gather.62 = bf16[2,8,64]{1,0,2:T(2,128)(2,1)S(1)} all-gather(bf16[2,8,4]{1,0,2:T(2,128)(2,1)S(1)} %get-tuple-element.616), channel_id=1, replica_groups=mesh['dp'=16,'tensor'=2] {'dp'}, dimensions={2}, use_global_device_ids=true | all-gather | bytes 2176 | tf_op jit(solution)/shard_map/while/body/eval_jaxpr/all_gather | solution.py:91
  165.5 47.4 %all-gather.17.cloned.1.call-done = bf16[3,1024,512]{2,1,0:T(8,128)(2,1)} async-done(((bf16[3,64,512]{2,1,0:T(8,128)(2,1)}), bf16[3,1024,512]{2,1,0:T(8,128)(2,1)}) %all-gather.17.cloned.1.call-update) | async-done | bytes 3145744 | tf_op jit(solution)/shard_map/while/body/eval_jaxpr/all_gather | solution.py:90
  223.9 28.0 %all-gather.19.cloned.1.call-done = bf16[512,1024]{0,1:T(8,128)(2,1)} async-done(((bf16[512,64]{0,1:T(8,128)(2,1)}), bf16[512,1024]{0,1:T(8,128)(2,1)}) %all-gather.19.cloned.1.call-update) | async-done | bytes 1048592 | tf_op jit(solution)/shard_map/while/body/eval_jaxpr/all_gather | solution.py:92
  255.6 18.7 %reduce-scatter.33.cloned.1.call-done = bf16[256,1024]{1,0:T(8,128)(2,1)} async-done(((bf16[512,1024]{1,0:T(8,128)(2,1)}), bf16[256,1024]{1,0:T(8,128)(2,1)}) %reduce-scatter.33.cloned.1.call-update) | async-done | bytes 524304 | tf_op jit(solution)/shard_map/while/body/eval_jaxpr/reduce_scatter | solution.py:109
  280.0 22.0 %all_gather.60 = bf16[1,2048]{1,0:T(2,128)(2,1)S(1)} all-gather(bf16[1,128]{1,0:T(2,128)(2,1)S(1)} %copy-done.14), channel_id=1, replica_groups=mesh['dp'=16,'tensor'=2] {'dp'}, dimensions={1}, use_global_device_ids=true | all-gather | bytes 4352 | tf_op jit(solution)/shard_map/while/body/eval_jaxpr/all_gather | solution.py:94
  301.9 25.2 %all-gather.23.cloned.1.call-done = bf16[1024,2048]{1,0:T(8,128)(2,1)} async-done(((bf16[64,2048]{1,0:T(8,128)(2,1)}), bf16[1024,2048]{1,0:T(8,128)(2,1)}) %all-gather.23.cloned.1.call-update) | async-done | bytes 4194320 | tf_op jit(solution)/shard_map/while/body/eval_jaxpr/all_gather | solution.py:93
  327.1 21.9 %all-gather.21.cloned.1.call-done = bf16[512,1024]{1,0:T(8,128)(2,1)} async-done(((bf16[256,1024]{1,0:T(8,128)(2,1)}), bf16[512,1024]{1,0:T(8,128)(2,1)}) %all-gather.21.cloned.1.call-update) | async-done | bytes 1048592 | tf_op jit(solution)/shard_map/while/body/eval_jaxpr/all_gather | solution.py:117
  349.0 15.2 multiply_convert_fusion.4
  364.2 37.9 %all-gather.25.cloned.1.call-done = bf16[2048,1024]{0,1:T(8,128)(2,1)} async-done(((bf16[2048,64]{0,1:T(8,128)(2,1)}), bf16[2048,1024]{0,1:T(8,128)(2,1)}) %all-gather.25.cloned.1.call-update) | async-done | bytes 4194320 | tf_op jit(solution)/shard_map/while/body/eval_jaxpr/all_gather | solution.py:95
  402.1 6.3 convolution_convert_fusion.9
  408.5 18.9 %reduce-scatter.35.cloned.1.call-done = bf16[256,1024]{1,0:T(8,128)(2,1)} async-done(((bf16[512,1024]{1,0:T(8,128)(2,1)}), bf16[256,1024]{1,0:T(8,128)(2,1)}) %reduce-scatter.35.cloned.1.call-update) | async-done | bytes 524304 | tf_op jit(solution)/shard_map/while/body/eval_jaxpr/reduce_scatter | solution.py:122
  433.6 21.3 %all-gather.27.cloned.1.call-done = bf16[512,1024]{1,0:T(8,128)(2,1)} async-done(((bf16[256,1024]{1,0:T(8,128)(2,1)}), bf16[512,1024]{1,0:T(8,128)(2,1)}) %all-gather.27.cloned.1.call-update) | async-done | bytes 1048592 | tf_op jit(solution)/shard_map/while/body/eval_jaxpr/all_gather | solution.py:143
  454.9 8.7 convert_reduce_fusion.6
  470.7 18.2 %reduce-scatter.37.cloned.1.call-done = bf16[256,1024]{1,0:T(8,128)(2,1)} async-done(((bf16[512,1024]{1,0:T(8,128)(2,1)}), bf16[256,1024]{1,0:T(8,128)(2,1)}) %reduce-scatter.37.cloned.1.call-update) | async-done | bytes 524304 | tf_op jit(solution)/shard_map/while/body/eval_jaxpr/reduce_scatter | solution.py:156
  494.0 7.7 select_add_fusion.11
  501.8 5.7 select_add_fusion.10
  507.4 7.8 all-gather.29.cloned.1.call-done
  543.2 12.2 reduce-scatter.39.cloned.1.call-done
  561.7 21.4 %all_gather.62 = bf16[2,8,64]{1,0,2:T(2,128)(2,1)S(1)} all-gather(bf16[2,8,4]{1,0,2:T(2,128)(2,1)S(1)} %get-tuple-element.616), channel_id=1, replica_groups=mesh['dp'=16,'tensor'=2] {'dp'}, dimensions={2}, use_global_device_ids=true | all-gather | bytes 2176 | tf_op jit(solution)/shard_map/while/body/eval_jaxpr/all_gather | solution.py:91
  583.5 45.9 %all-gather.17.cloned.1.call-done = bf16[3,1024,512]{2,1,0:T(8,128)(2,1)} async-done(((bf16[3,64,512]{2,1,0:T(8,128)(2,1)}), bf16[3,1024,512]{2,1,0:T(8,128)(2,1)}) %all-gather.17.cloned.1.call-update) | async-done | bytes 3145744 | tf_op jit(solution)/shard_map/while/body/eval_jaxpr/all_gather | solution.py:90
  640.4 27.8 %all-gather.19.cloned.1.call-done = bf16[512,1024]{0,1:T(8,128)(2,1)} async-done(((bf16[512,64]{0,1:T(8,128)(2,1)}), bf16[512,1024]{0,1:T(8,128)(2,1)}) %all-gather.19.cloned.1.call-update) | async-done | bytes 1048592 | tf_op jit(solution)/shard_map/while/body/eval_jaxpr/all_gather | solution.py:92
  671.9 18.7 %reduce-scatter.33.cloned.1.call-done = bf16[256,1024]{1,0:T(8,128)(2,1)} async-done(((bf16[512,1024]{1,0:T(8,128)(2,1)}), bf16[256,1024]{1,0:T(8,128)(2,1)}) %reduce-scatter.33.cloned.1.call-update) | async-done | bytes 524304 | tf_op jit(solution)/shard_map/while/body/eval_jaxpr/reduce_scatter | solution.py:109
  696.3 21.5 %all_gather.60 = bf16[1,2048]{1,0:T(2,128)(2,1)S(1)} all-gather(bf16[1,128]{1,0:T(2,128)(2,1)S(1)} %copy-done.14), channel_id=1, replica_groups=mesh['dp'=16,'tensor'=2] {'dp'}, dimensions={1}, use_global_device_ids=true | all-gather | bytes 4352 | tf_op jit(solution)/shard_map/while/body/eval_jaxpr/all_gather | solution.py:94
  717.8 25.7 %all-gather.23.cloned.1.call-done = bf16[1024,2048]{1,0:T(8,128)(2,1)} async-done(((bf16[64,2048]{1,0:T(8,128)(2,1)}), bf16[1024,2048]{1,0:T(8,128)(2,1)}) %all-gather.23.cloned.1.call-update) | async-done | bytes 4194320 | tf_op jit(solution)/shard_map/while/body/eval_jaxpr/all_gather | solution.py:93
  743.5 21.9 %all-gather.21.cloned.1.call-done = bf16[512,1024]{1,0:T(8,128)(2,1)} async-done(((bf16[256,1024]{1,0:T(8,128)(2,1)}), bf16[512,1024]{1,0:T(8,128)(2,1)}) %all-gather.21.cloned.1.call-update) | async-done | bytes 1048592 | tf_op jit(solution)/shard_map/while/body/eval_jaxpr/all_gather | solution.py:117
  765.3 15.2 multiply_convert_fusion.4
  780.6 37.9 %all-gather.25.cloned.1.call-done = bf16[2048,1024]{0,1:T(8,128)(2,1)} async-done(((bf16[2048,64]{0,1:T(8,128)(2,1)}), bf16[2048,1024]{0,1:T(8,128)(2,1)}) %all-gather.25.cloned.1.call-update) | async-done | bytes 4194320 | tf_op jit(solution)/shard_map/while/body/eval_jaxpr/all_gather | solution.py:95
  818.5 6.2 convolution_convert_fusion.9
  824.8 18.9 %reduce-scatter.35.cloned.1.call-done = bf16[256,1024]{1,0:T(8,128)(2,1)} async-done(((bf16[512,1024]{1,0:T(8,128)(2,1)}), bf16[256,1024]{1,0:T(8,128)(2,1)}) %reduce-scatter.35.cloned.1.call-update) | async-done | bytes 524304 | tf_op jit(solution)/shard_map/while/body/eval_jaxpr/reduce_scatter | solution.py:122
  850.0 21.2 %all-gather.27.cloned.1.call-done = bf16[512,1024]{1,0:T(8,128)(2,1)} async-done(((bf16[256,1024]{1,0:T(8,128)(2,1)}), bf16[512,1024]{1,0:T(8,128)(2,1)}) %all-gather.27.cloned.1.call-update) | async-done | bytes 1048592 | tf_op jit(solution)/shard_map/while/body/eval_jaxpr/all_gather | solution.py:143
  871.2 8.7 convert_reduce_fusion.6
  887.0 18.2 %reduce-scatter.37.cloned.1.call-done = bf16[256,1024]{1,0:T(8,128)(2,1)} async-done(((bf16[512,1024]{1,0:T(8,128)(2,1)}), bf16[256,1024]{1,0:T(8,128)(2,1)}) %reduce-scatter.37.cloned.1.call-update) | async-done | bytes 524304 | tf_op jit(solution)/shard_map/while/body/eval_jaxpr/reduce_scatter | solution.py:156
  910.4 10.1 select_add_fusion.11
  920.5 9.1 select_add_fusion.10
  956.1 7.7 bitcast_add_fusion.2
  963.7 8.3 reduce-scatter.39.cloned.1.call-done
  987.3 6.0 convert_element_type.143
  993.4 7.4 copy.56
  1002.7 61.3 %all-reduce = bf16[2,8,64]{1,2,0:T(8,128)(2,1)S(1)} all-reduce(bf16[2,8,64]{1,2,0:T(8,128)(2,1)S(1)} %copy.54), channel_id=8, replica_groups=mesh['dp'=16,'tensor'=2] {'dp'}, use_global_device_ids=true, to_apply=%region_26.27.clone | all-reduce | flops 1024 | bytes 4096
  1066.0 107.1 %reduce-scatter.29.cloned.1.call-done = f32[32,2]{1,0:T(8,128)} async-done(((f32[1024,2]{1,0:T(8,128)}), f32[32,2]{1,0:T(8,128)}) %reduce-scatter.29.cloned.1.call-update) | async-done | bytes 272
  1174.5 130.3 %reduce-scatter.31.cloned.1.call-done = f32[32,4]{1,0:T(8,128)} async-done(((f32[1024,4]{1,0:T(8,128)}), f32[32,4]{1,0:T(8,128)}) %reduce-scatter.31.cloned.1.call-update) | async-done | bytes 528
  1306.1 56.1 %reduce-scatter.21.cloned.1.call-done = bf16[512,64]{0,1:T(8,128)(2,1)} async-done(((bf16[512,1024]{0,1:T(8,128)(2,1)}), bf16[512,64]{0,1:T(8,128)(2,1)}) %reduce-scatter.21.cloned.1.call-update) | async-done | bytes 65552 | tf_op jit(solution)/shard_map/reduce_scatter | solution.py:234
  1363.7 67.5 %reduce-scatter.19.cloned.1.call-done = bf16[3,64,512]{2,1,0:T(8,128)(2,1)} async-done(((bf16[3,1024,512]{2,1,0:T(8,128)(2,1)}), bf16[3,64,512]{2,1,0:T(8,128)(2,1)}) %reduce-scatter.19.cloned.1.call-update) | async-done | bytes 196624 | tf_op jit(solution)/shard_map/reduce_scatter | solution.py:228
  1433.0 73.4 %reduce-scatter.23.cloned.1.call-done = bf16[64,2048]{1,0:T(8,128)(2,1)} async-done(((bf16[1024,2048]{1,0:T(8,128)(2,1)}), bf16[64,2048]{1,0:T(8,128)(2,1)}) %reduce-scatter.23.cloned.1.call-update) | async-done | bytes 262160 | tf_op jit(solution)/shard_map/reduce_scatter | solution.py:237
  1508.1 73.9 %reduce-scatter.25.cloned.1.call-done = bf16[2048,64]{0,1:T(8,128)(2,1)} async-done(((bf16[2048,1024]{0,1:T(8,128)(2,1)}), bf16[2048,64]{0,1:T(8,128)(2,1)}) %reduce-scatter.25.cloned.1.call-update) | async-done | bytes 262160 | tf_op jit(solution)/shard_map/reduce_scatter | solution.py:243
  (286 shorter events, 168.5 us)
Async XLA Ops:
  143.2 22.3 %all-gather.15.cloned.1.call-start = ((), (), s32[]{:S(2)}) async-start(), calls=%async_computation.18 | async-start | bytes 1572864 | tf_op jit(solution)/shard_map/while/body/eval_jaxpr/all_gather | solution.py:97
  145.2 67.8 %all-gather.17.cloned.1.call-start = ((), (), s32[]{:S(2)}) async-start(), calls=%async_computation.19 | async-start | bytes 3342336 | tf_op jit(solution)/shard_map/while/body/eval_jaxpr/all_gather | solution.py:90
  145.9 106.0 %all-gather.19.cloned.1.call-start = ((), (), s32[]{:S(2)}) async-start(), calls=%async_computation.20 | async-start | bytes 1114112 | tf_op jit(solution)/shard_map/while/body/eval_jaxpr/all_gather | solution.py:92
  146.6 127.6 %reduce-scatter.33.cloned.1.call-start = ((), (), s32[]{:S(2)}) async-start(), calls=%async_computation.21 | async-start | bytes 1572864 | tf_op jit(solution)/shard_map/while/body/eval_jaxpr/reduce_scatter | solution.py:109
  223.9 55.3 %copy-start.12 = (bf16[8,64,512]{2,1,0:T(8,128)(2,1)}, bf16[8,64,512]{2,1,0:T(8,128)(2,1)S(1)}, u32[]{:S(2)}) copy-start(bf16[8,64,512]{2,1,0:T(8,128)(2,1)S(1)} %fusion.158) | copy-start | bytes 1572868 | tf_op jit(solution)/shard_map/while
  223.9 50.4 %copy-start.2 = (bf16[2,256,1024]{2,1,0:T(8,128)(2,1)S(1)}, bf16[2,256,1024]{2,1,0:T(8,128)(2,1)}, u32[]{:S(2)}) copy-start(bf16[2,256,1024]{2,1,0:T(8,128)(2,1)} %get-tuple-element.613) | copy-start | bytes 3145732 | tf_op jit(solution)/shard_map/while
  251.9 28.1 %copy-start.14 = (bf16[1,128]{1,0:T(2,128)(2,1)S(1)}, bf16[1,128]{1,0:T(2,128)(2,1)}, u32[]{:S(2)}) copy-start(bf16[1,128]{1,0:T(2,128)(2,1)} %get-tuple-element.621) | copy-start | bytes 772 | tf_op jit(solution)/shard_map/while
  254.9 72.2 %all-gather.23.cloned.1.call-start = ((), (), s32[]{:S(2)}) async-start(), calls=%async_computation.23 | async-start | bytes 4456448 | tf_op jit(solution)/shard_map/while/body/eval_jaxpr/all_gather | solution.py:93
  255.5 93.5 %all-gather.21.cloned.1.call-start = ((), (), s32[]{:S(2)}) async-start(), calls=%async_computation.22 | async-start | bytes 1572864 | tf_op jit(solution)/shard_map/while/body/eval_jaxpr/all_gather | solution.py:117
  279.1 123.0 %all-gather.25.cloned.1.call-start = ((), (), s32[]{:S(2)}) async-start(), calls=%async_computation.24 | async-start | bytes 4456448 | tf_op jit(solution)/shard_map/while/body/eval_jaxpr/all_gather | solution.py:95
  279.9 147.5 %reduce-scatter.35.cloned.1.call-start = ((), (), s32[]{:S(2)}) async-start(), calls=%async_computation.25 | async-start | bytes 1572864 | tf_op jit(solution)/shard_map/while/body/eval_jaxpr/reduce_scatter | solution.py:122
  402.1 25.2 %copy-start.1 = (bf16[256,1024]{1,0:T(8,128)(2,1)S(1)}, bf16[256,1024]{1,0:T(8,128)(2,1)}, u32[]{:S(2)}) copy-start(bf16[256,1024]{1,0:T(8,128)(2,1)} %reduce-scatter.33.cloned.1.call-done) | copy-start | bytes 1572868 | tf_op jit(solution)/shard_map/while
  408.4 46.5 %all-gather.27.cloned.1.call-start = ((), (), s32[]{:S(2)}) async-start(), calls=%async_computation.26 | async-start | bytes 1572864 | tf_op jit(solution)/shard_map/while/body/eval_jaxpr/all_gather | solution.py:143
  433.4 55.5 %reduce-scatter.37.cloned.1.call-start = ((), (), s32[]{:S(2)}) async-start(), calls=%async_computation.27 | async-start | bytes 1572864 | tf_op jit(solution)/shard_map/while/body/eval_jaxpr/reduce_scatter | solution.py:156
  454.9 10.1 copy-start.15
  468.4 46.8 %all-gather.29.cloned.1.call-start = ((), (), s32[]{:S(2)}) async-start(), calls=%async_computation.28 | async-start | bytes 1572864 | tf_op jit(solution)/shard_map/while/body/eval_jaxpr/all_gather | solution.py:168
  493.8 61.6 %reduce-scatter.39.cloned.1.call-start = ((), (), s32[]{:S(2)}) async-start(), calls=%async_computation.29 | async-start | bytes 1572864 | tf_op jit(solution)/shard_map/while/body/eval_jaxpr/reduce_scatter | solution.py:190
  494.0 7.7 copy-start.8
  501.7 13.5 copy-start.17
  517.2 9.9 slice-start
  557.8 25.7 %all-gather.15.cloned.1.call-start = ((), (), s32[]{:S(2)}) async-start(), calls=%async_computation.18 | async-start | bytes 1572864 | tf_op jit(solution)/shard_map/while/body/eval_jaxpr/all_gather | solution.py:97
  559.8 69.6 %all-gather.17.cloned.1.call-start = ((), (), s32[]{:S(2)}) async-start(), calls=%async_computation.19 | async-start | bytes 3342336 | tf_op jit(solution)/shard_map/while/body/eval_jaxpr/all_gather | solution.py:90
  560.4 107.9 %all-gather.19.cloned.1.call-start = ((), (), s32[]{:S(2)}) async-start(), calls=%async_computation.20 | async-start | bytes 1114112 | tf_op jit(solution)/shard_map/while/body/eval_jaxpr/all_gather | solution.py:92
  561.0 129.7 %reduce-scatter.33.cloned.1.call-start = ((), (), s32[]{:S(2)}) async-start(), calls=%async_computation.21 | async-start | bytes 1572864 | tf_op jit(solution)/shard_map/while/body/eval_jaxpr/reduce_scatter | solution.py:109
  640.4 55.1 %copy-start.12 = (bf16[8,64,512]{2,1,0:T(8,128)(2,1)}, bf16[8,64,512]{2,1,0:T(8,128)(2,1)S(1)}, u32[]{:S(2)}) copy-start(bf16[8,64,512]{2,1,0:T(8,128)(2,1)S(1)} %fusion.158) | copy-start | bytes 1572868 | tf_op jit(solution)/shard_map/while
  640.4 50.2 %copy-start.2 = (bf16[2,256,1024]{2,1,0:T(8,128)(2,1)S(1)}, bf16[2,256,1024]{2,1,0:T(8,128)(2,1)}, u32[]{:S(2)}) copy-start(bf16[2,256,1024]{2,1,0:T(8,128)(2,1)} %get-tuple-element.613) | copy-start | bytes 3145732 | tf_op jit(solution)/shard_map/while
  668.2 28.1 %copy-start.14 = (bf16[1,128]{1,0:T(2,128)(2,1)S(1)}, bf16[1,128]{1,0:T(2,128)(2,1)}, u32[]{:S(2)}) copy-start(bf16[1,128]{1,0:T(2,128)(2,1)} %get-tuple-element.621) | copy-start | bytes 772 | tf_op jit(solution)/shard_map/while
  671.2 72.2 %all-gather.23.cloned.1.call-start = ((), (), s32[]{:S(2)}) async-start(), calls=%async_computation.23 | async-start | bytes 4456448 | tf_op jit(solution)/shard_map/while/body/eval_jaxpr/all_gather | solution.py:93
  671.8 93.5 %all-gather.21.cloned.1.call-start = ((), (), s32[]{:S(2)}) async-start(), calls=%async_computation.22 | async-start | bytes 1572864 | tf_op jit(solution)/shard_map/while/body/eval_jaxpr/all_gather | solution.py:117
  695.5 123.0 %all-gather.25.cloned.1.call-start = ((), (), s32[]{:S(2)}) async-start(), calls=%async_computation.24 | async-start | bytes 4456448 | tf_op jit(solution)/shard_map/while/body/eval_jaxpr/all_gather | solution.py:95
  696.3 147.5 %reduce-scatter.35.cloned.1.call-start = ((), (), s32[]{:S(2)}) async-start(), calls=%async_computation.25 | async-start | bytes 1572864 | tf_op jit(solution)/shard_map/while/body/eval_jaxpr/reduce_scatter | solution.py:122
  818.5 25.2 %copy-start.1 = (bf16[256,1024]{1,0:T(8,128)(2,1)S(1)}, bf16[256,1024]{1,0:T(8,128)(2,1)}, u32[]{:S(2)}) copy-start(bf16[256,1024]{1,0:T(8,128)(2,1)} %reduce-scatter.33.cloned.1.call-done) | copy-start | bytes 1572868 | tf_op jit(solution)/shard_map/while
  824.8 46.5 %all-gather.27.cloned.1.call-start = ((), (), s32[]{:S(2)}) async-start(), calls=%async_computation.26 | async-start | bytes 1572864 | tf_op jit(solution)/shard_map/while/body/eval_jaxpr/all_gather | solution.py:143
  849.7 55.5 %reduce-scatter.37.cloned.1.call-start = ((), (), s32[]{:S(2)}) async-start(), calls=%async_computation.27 | async-start | bytes 1572864 | tf_op jit(solution)/shard_map/while/body/eval_jaxpr/reduce_scatter | solution.py:156
  871.2 10.1 copy-start.15
  884.7 46.8 %all-gather.29.cloned.1.call-start = ((), (), s32[]{:S(2)}) async-start(), calls=%async_computation.28 | async-start | bytes 1572864 | tf_op jit(solution)/shard_map/while/body/eval_jaxpr/all_gather | solution.py:168
  910.1 61.9 %reduce-scatter.39.cloned.1.call-start = ((), (), s32[]{:S(2)}) async-start(), calls=%async_computation.29 | async-start | bytes 1572864 | tf_op jit(solution)/shard_map/while/body/eval_jaxpr/reduce_scatter | solution.py:190
  910.4 10.1 copy-start.8
  910.4 10.1 copy-start.10
  920.5 11.0 copy-start.17
  933.6 10.2 slice-start
  976.9 87.7 %reduce-scatter.27.cloned.1.call-start = ((), (), s32[]{:S(2)}) async-start(), calls=%async_computation.15 | async-start | bytes 557056
  978.0 195.1 %reduce-scatter.29.cloned.1.call-start = ((), (), s32[]{:S(2)}) async-start(), calls=%async_computation.16 | async-start | bytes 540672
  979.2 325.6 %reduce-scatter.31.cloned.1.call-start = ((), (), s32[]{:S(2)}) async-start(), calls=%async_computation.17 | async-start | bytes 540672
  980.3 381.9 %reduce-scatter.21.cloned.1.call-start = ((), (), s32[]{:S(2)}) async-start(), calls=%async_computation.12 | async-start | bytes 1114112 | tf_op jit(solution)/shard_map/reduce_scatter | solution.py:234
  981.8 449.5 %reduce-scatter.19.cloned.1.call-start = ((), (), s32[]{:S(2)}) async-start(), calls=%async_computation.11 | async-start | bytes 3342336 | tf_op jit(solution)/shard_map/reduce_scatter | solution.py:228
  987.3 519.1 %reduce-scatter.23.cloned.1.call-start = ((), (), s32[]{:S(2)}) async-start(), calls=%async_computation.13 | async-start | bytes 4456448 | tf_op jit(solution)/shard_map/reduce_scatter | solution.py:237
  993.4 588.7 %reduce-scatter.25.cloned.1.call-start = ((), (), s32[]{:S(2)}) async-start(), calls=%async_computation.14 | async-start | bytes 4456448 | tf_op jit(solution)/shard_map/reduce_scatter | solution.py:243
  (23 other events, 73.9 us)
Sparse Core Ops, SparseCore 0:
  146.2 19.2 all-gather.14
  167.7 45.1 all-gather.16
  215.1 36.7 all-gather.18
  255.0 19.2 reduce-scatter.32
  276.5 50.5 all-gather.22
  329.2 19.7 all-gather.20
  351.4 50.7 all-gather.24
  408.5 18.7 reduce-scatter.34
  433.5 21.3 all-gather.26
  468.5 20.3 reduce-scatter.36
  493.9 21.2 all-gather.28
  535.1 20.3 reduce-scatter.38
  560.8 21.2 all-gather.14
  584.2 45.1 all-gather.16
  631.4 36.7 all-gather.18
  671.4 19.2 reduce-scatter.32
  692.9 50.5 all-gather.22
  745.5 19.7 all-gather.20
  767.7 50.7 all-gather.24
  824.9 18.7 reduce-scatter.34
  849.9 21.3 all-gather.26
  884.9 20.3 reduce-scatter.36
  910.2 21.2 all-gather.28
  951.7 20.3 reduce-scatter.38
Sparse Core Ops, SparseCore 1:
  981.5 55.8 reduce-scatter.26
  1040.1 132.9 reduce-scatter.28
  1175.2 129.5 reduce-scatter.30
  1308.8 53.4 reduce-scatter.20
  1366.0 65.1 reduce-scatter.18
  1435.1 71.1 reduce-scatter.22
  1510.5 71.4 reduce-scatter.24
where the time goes:
time: 1590 us
  waiting for transfers between devices  1020 us (64%)
  blocking collectives  277 us (17%)
  matrix products  174 us (11%)
  other arithmetic  62.4 us (4%)
  local copies, waits for them, and re-layouts  35.9 us (2%)
  between operations  16.6 us (1%)
    unnamed x10, waiting for transfers between devices  238 us
    all_gather x2, waiting for transfers between devices, micro_step(): lax.all_gather(shards[0], 'dp', axis=1, tiled=True)  93.3 us
    all_gather x2, waiting for transfers between devices, micro_step(): lax.all_gather(shards[5], 'dp', axis=1, tiled=True)  75.8 us
    reduce_scatter x1, waiting for transfers between devices, local(): lax.psum_scatter(totals[5].astype(jnp.bfloat16), 'dp', scatter_dimension=...  73.9 us
    reduce_scatter x1, waiting for transfers between devices, local(): lax.psum_scatter(totals[3].astype(jnp.bfloat16), 'dp', scatter_dimension=...  73.4 us
    all_gather x1, blocking collectives, local(): lax.all_gather(norm_gains, ('dp', 'tensor'), axis=1, tiled=True)  70 us
    reduce_scatter x1, waiting for transfers between devices, local(): lax.psum_scatter(totals[0].astype(jnp.bfloat16), 'dp', scatter_dimension=...  67.5 us
    all_gather x1, blocking collectives, local(): lax.all_gather(row_biases, ('dp', 'tensor'), axis=1, tiled=True)  63.9 us
  transfers between devices with their start and end apart: 31, of which 29 were waited for; matrix products, arithmetic and copies ran while one was open for 9% of the time, Pallas kernels for 0%

commit v1 on v0

--- a/solution.py
+++ b/solution.py
@@ -4,6 +4,19 @@
 from jax.sharding import PartitionSpec as P
 
 HEAD_DIM = 64
+
+
+def gather_around(array, axis, dim):
+    ways = lax.axis_size(axis)
+    up = [(d, (d + 1) % ways) for d in range(ways)]
+    down = [(d, (d - 1) % ways) for d in range(ways)]
+    earlier, later = ([array], [array])
+    for _ in range(ways // 2):
+        earlier.append(lax.ppermute(earlier[-1], axis, up))
+    for _ in range((ways - 1) // 2):
+        later.append(lax.ppermute(later[-1], axis, down))
+    line = jnp.concatenate([*earlier[::-1], *later[1:]], axis=dim)
+    return jnp.roll(line, (lax.axis_index(axis) - ways // 2) * array.shape[dim], axis=dim)
 
 
 def gelu_exact(values):
@@ -89,7 +102,7 @@
         qkv_full, qv_full, out_full, up_full, upb_full, down_full = (
             lax.all_gather(shards[0], "dp", axis=1, tiled=True),
             lax.all_gather(shards[1], "dp", axis=2, tiled=True),
-            lax.all_gather(shards[2], "dp", axis=1, tiled=True),
+            gather_around(shards[2], "dp", 1),
             lax.all_gather(shards[3], "dp", axis=0, tiled=True),
             lax.all_gather(shards[4], "dp", axis=1, tiled=True),
             lax.all_gather(shards[5], "dp", axis=1, tiled=True),

time: 1590 us -> 1670 us (1.050)
  starting transfers between devices: 2.18 us -> 34.5 us
  waiting for transfers between devices: 1020 us -> 1050 us
    all_gather x2, waiting for transfers between devices: 9.74 us -> 44.9 us  [micro_step(): lax.all_gather(grad_one.astype(jnp.bfloat16), 'tensor', axis=0, tiled=True)]
    ppermute x0 -> x15, starting transfers between devices: none -> 32.3 us  [the longest x7 31.8 us: gather_around(): later.append(lax.ppermute(later[-1], axis, down))]
    ppermute x0 -> x15, waiting for transfers between devices: none -> 18.9 us  [the longest x8 18.9 us: gather_around(): earlier.append(lax.ppermute(earlier[-1], axis, up))]
    all_gather x2, waiting for transfers between devices: 55.8 us -> 37.6 us  [micro_step(): lax.all_gather(shards[2], 'dp', axis=1, tiled=True)]
  transfers between devices with their start and end apart: 31 -> 46, of which waited for: 29 -> 37; matrix products, arithmetic and copies ran while one was open for 9% -> 9% of each run, Pallas kernels for 0% -> 0%
where the time goes in v1:
time: 1670 us
  waiting for transfers between devices  1050 us (63%)
  blocking collectives  277 us (17%)
  matrix products  173 us (10%)
  other arithmetic  64.5 us (4%)
  local copies, waits for them, and re-layouts  43.8 us (3%)
  starting transfers between devices  34.5 us (2%)
    unnamed x10, waiting for transfers between devices  237 us
    all_gather x2, waiting for transfers between devices, micro_step(): lax.all_gather(shards[0], 'dp', axis=1, tiled=True)  94.7 us
    all_gather x2, waiting for transfers between devices, micro_step(): lax.all_gather(shards[5], 'dp', axis=1, tiled=True)  75.4 us
    reduce_scatter x1, waiting for transfers between devices, local(): lax.psum_scatter(totals[5].astype(jnp.bfloat16), 'dp', scatter_dimension=...  73.8 us
    reduce_scatter x1, waiting for transfers between devices, local(): lax.psum_scatter(totals[3].astype(jnp.bfloat16), 'dp', scatter_dimension=...  73.3 us
    all_gather x1, blocking collectives, local(): lax.all_gather(norm_gains, ('dp', 'tensor'), axis=1, tiled=True)  69.4 us
    reduce_scatter x1, waiting for transfers between devices, local(): lax.psum_scatter(totals[0].astype(jnp.bfloat16), 'dp', scatter_dimension=...  67.5 us
    all_gather x1, blocking collectives, local(): lax.all_gather(row_biases, ('dp', 'tensor'), axis=1, tiled=True)  63.9 us
  transfers between devices with their start and end apart: 46, of which 37 were waited for; matrix products, arithmetic and copies ran while one was open for 9% of the time, Pallas kernels for 0%

profile of v1, /device:TPU:0, one launch (start us, length us, event | category | flops | bytes accessed | tf_op | source)
XLA Modules:
  0.0 1667.8 jit_solution(15551771960357355896)
XLA Ops:
  61.0 69.4 %all-gather.2 = f32[32,32,2]{1,2,0:T(2,128)S(1)} all-gather(f32[1,32,2]{1,2,0:T(2,128)} %bitcast.319), channel_id=1, replica_groups=mesh['dp'=16,'tensor'=2] {'dp','tensor'}, dimensions={0}, use_global_device_ids=true | all-gather | bytes 8448 | tf_op jit(solution)/shard_map/all_gather | solution.py:90
  130.6 63.9 %all-gather.1 = f32[32,32,4]{1,2,0:T(4,128)S(1)} all-gather(f32[1,32,4]{1,2,0:T(4,128)} %bitcast.318), channel_id=1, replica_groups=mesh['dp'=16,'tensor'=2] {'dp','tensor'}, dimensions={0}, use_global_device_ids=true | all-gather | bytes 16896 | tf_op jit(solution)/shard_map/all_gather | solution.py:91
  194.6 8.5 concatenate.13
  203.2 850.5 %while.31 = (s32[]{:T(128)}, f32[3,1024,512]{1,2,0:T(8,128)}, f32[2,8,64]{2,1,0:T(8,128)S(1)}, f32[512,1024]{1,0:T(8,128)}, f32[1024,2048]{1,0:T(8,128)}, /*inde...) while((s32[]{:T(128)}, f32[3,1024,512]{1,2,0:T(8,128)}, ...), condition=%wide.region_24.25_spmd.clone, body=%wide.region_0.24_spmd.clone.sunk | while | flops 21109161984 | bytes 474818496 | solution.py:237
  205.4 17.2 %all_gather.91 = bf16[2,8,64]{1,0,2:T(2,128)(2,1)S(1)} all-gather(bf16[2,8,4]{1,0,2:T(2,128)(2,1)S(1)} %get-tuple-element.827), channel_id=1, replica_groups=mesh['dp'=16,'tensor'=2] {'dp'}, dimensions={2}, use_global_device_ids=true | all-gather | bytes 2176 | tf_op jit(solution)/shard_map/while/body/eval_jaxpr/all_gather | solution.py:104
  225.9 47.4 %all-gather.17.cloned.1.call-done = bf16[3,1024,512]{2,1,0:T(8,128)(2,1)} async-done(((bf16[3,64,512]{2,1,0:T(8,128)(2,1)}), bf16[3,1024,512]{2,1,0:T(8,128)(2,1)}) %all-gather.17.cloned.1.call-update) | async-done | bytes 3145744 | tf_op jit(solution)/shard_map/while/body/eval_jaxpr/all_gather | solution.py:103
  286.9 18.6 %reduce-scatter.33.cloned.1.call-done = bf16[256,1024]{1,0:T(8,128)(2,1)} async-done(((bf16[512,1024]{1,0:T(8,128)(2,1)}), bf16[256,1024]{1,0:T(8,128)(2,1)}) %reduce-scatter.33.cloned.1.call-update) | async-done | bytes 524304 | tf_op jit(solution)/shard_map/while/body/eval_jaxpr/reduce_scatter | solution.py:122
  311.0 21.7 %all_gather.89 = bf16[1,2048]{1,0:T(2,128)(2,1)S(1)} all-gather(bf16[1,128]{1,0:T(2,128)(2,1)S(1)} %get-tuple-element.832), channel_id=1, replica_groups=mesh['dp'=16,'tensor'=2] {'dp'}, dimensions={1}, use_global_device_ids=true | all-gather | bytes 4352 | tf_op jit(solution)/shard_map/while/body/eval_jaxpr/all_gather | solution.py:107
  332.8 25.6 %all-gather.21.cloned.1.call-done = bf16[1024,2048]{1,0:T(8,128)(2,1)} async-done(((bf16[64,2048]{1,0:T(8,128)(2,1)}), bf16[1024,2048]{1,0:T(8,128)(2,1)}) %all-gather.21.cloned.1.call-update) | async-done | bytes 4194320 | tf_op jit(solution)/shard_map/while/body/eval_jaxpr/all_gather | solution.py:106
  358.4 21.9 %all-gather.19.cloned.1.call-done = bf16[512,1024]{1,0:T(8,128)(2,1)} async-done(((bf16[256,1024]{1,0:T(8,128)(2,1)}), bf16[512,1024]{1,0:T(8,128)(2,1)}) %all-gather.19.cloned.1.call-update) | async-done | bytes 1048592 | tf_op jit(solution)/shard_map/while/body/eval_jaxpr/all_gather | solution.py:130
  380.3 15.2 multiply_convert_fusion.4
  395.5 37.6 %all-gather.23.cloned.1.call-done = bf16[2048,1024]{0,1:T(8,128)(2,1)} async-done(((bf16[2048,64]{0,1:T(8,128)(2,1)}), bf16[2048,1024]{0,1:T(8,128)(2,1)}) %all-gather.23.cloned.1.call-update) | async-done | bytes 4194320 | tf_op jit(solution)/shard_map/while/body/eval_jaxpr/all_gather | solution.py:108
  433.1 6.2 convolution_convert_fusion.9
  439.4 18.9 %reduce-scatter.35.cloned.1.call-done = bf16[256,1024]{1,0:T(8,128)(2,1)} async-done(((bf16[512,1024]{1,0:T(8,128)(2,1)}), bf16[256,1024]{1,0:T(8,128)(2,1)}) %reduce-scatter.35.cloned.1.call-update) | async-done | bytes 524304 | tf_op jit(solution)/shard_map/while/body/eval_jaxpr/reduce_scatter | solution.py:135
  464.5 21.3 %all-gather.25.cloned.1.call-done = bf16[512,1024]{1,0:T(8,128)(2,1)} async-done(((bf16[256,1024]{1,0:T(8,128)(2,1)}), bf16[512,1024]{1,0:T(8,128)(2,1)}) %all-gather.25.cloned.1.call-update) | async-done | bytes 1048592 | tf_op jit(solution)/shard_map/while/body/eval_jaxpr/all_gather | solution.py:156
  485.8 8.7 convert_reduce_fusion.6
  502.2 17.6 %reduce-scatter.37.cloned.1.call-done = bf16[256,1024]{1,0:T(8,128)(2,1)} async-done(((bf16[512,1024]{1,0:T(8,128)(2,1)}), bf16[256,1024]{1,0:T(8,128)(2,1)}) %reduce-scatter.37.cloned.1.call-update) | async-done | bytes 524304 | tf_op jit(solution)/shard_map/while/body/eval_jaxpr/reduce_scatter | solution.py:169
  525.0 7.7 select_add_fusion.11
  538.3 21.7 %all-gather.29.cloned.1.call-done = bf16[512,1024]{0,1:T(8,128)(2,1)} async-done(((bf16[512,64]{0,1:T(8,128)(2,1)}), bf16[512,1024]{0,1:T(8,128)(2,1)}) %all-gather.29.cloned.1.call-update) | async-done | bytes 1048592 | tf_op jit(solution)/shard_map/while/body/eval_jaxpr/all_gather | solution.py:146
  560.0 22.5 %all-gather.27.cloned.1.call-done = bf16[512,1024]{1,0:T(8,128)(2,1)} async-done(((bf16[256,1024]{1,0:T(8,128)(2,1)}), bf16[512,1024]{1,0:T(8,128)(2,1)}) %all-gather.27.cloned.1.call-update) | async-done | bytes 1048592 | tf_op jit(solution)/shard_map/while/body/eval_jaxpr/all_gather | solution.py:181
  612.9 10.9 reduce-scatter.39.cloned.1.call-done
  627.8 21.4 %all_gather.91 = bf16[2,8,64]{1,0,2:T(2,128)(2,1)S(1)} all-gather(bf16[2,8,4]{1,0,2:T(2,128)(2,1)S(1)} %get-tuple-element.827), channel_id=1, replica_groups=mesh['dp'=16,'tensor'=2] {'dp'}, dimensions={2}, use_global_device_ids=true | all-gather | bytes 2176 | tf_op jit(solution)/shard_map/while/body/eval_jaxpr/all_gather | solution.py:104
  650.5 47.3 %all-gather.17.cloned.1.call-done = bf16[3,1024,512]{2,1,0:T(8,128)(2,1)} async-done(((bf16[3,64,512]{2,1,0:T(8,128)(2,1)}), bf16[3,1024,512]{2,1,0:T(8,128)(2,1)}) %all-gather.17.cloned.1.call-update) | async-done | bytes 3145744 | tf_op jit(solution)/shard_map/while/body/eval_jaxpr/all_gather | solution.py:103
  711.4 18.6 %reduce-scatter.33.cloned.1.call-done = bf16[256,1024]{1,0:T(8,128)(2,1)} async-done(((bf16[512,1024]{1,0:T(8,128)(2,1)}), bf16[256,1024]{1,0:T(8,128)(2,1)}) %reduce-scatter.33.cloned.1.call-update) | async-done | bytes 524304 | tf_op jit(solution)/shard_map/while/body/eval_jaxpr/reduce_scatter | solution.py:122
  735.5 21.5 %all_gather.89 = bf16[1,2048]{1,0:T(2,128)(2,1)S(1)} all-gather(bf16[1,128]{1,0:T(2,128)(2,1)S(1)} %get-tuple-element.832), channel_id=1, replica_groups=mesh['dp'=16,'tensor'=2] {'dp'}, dimensions={1}, use_global_device_ids=true | all-gather | bytes 4352 | tf_op jit(solution)/shard_map/while/body/eval_jaxpr/all_gather | solution.py:107
  757.0 25.9 %all-gather.21.cloned.1.call-done = bf16[1024,2048]{1,0:T(8,128)(2,1)} async-done(((bf16[64,2048]{1,0:T(8,128)(2,1)}), bf16[1024,2048]{1,0:T(8,128)(2,1)}) %all-gather.21.cloned.1.call-update) | async-done | bytes 4194320 | tf_op jit(solution)/shard_map/while/body/eval_jaxpr/all_gather | solution.py:106
  782.9 21.9 %all-gather.19.cloned.1.call-done = bf16[512,1024]{1,0:T(8,128)(2,1)} async-done(((bf16[256,1024]{1,0:T(8,128)(2,1)}), bf16[512,1024]{1,0:T(8,128)(2,1)}) %all-gather.19.cloned.1.call-update) | async-done | bytes 1048592 | tf_op jit(solution)/shard_map/while/body/eval_jaxpr/all_gather | solution.py:130
  804.8 15.2 multiply_convert_fusion.4
  820.0 37.8 %all-gather.23.cloned.1.call-done = bf16[2048,1024]{0,1:T(8,128)(2,1)} async-done(((bf16[2048,64]{0,1:T(8,128)(2,1)}), bf16[2048,1024]{0,1:T(8,128)(2,1)}) %all-gather.23.cloned.1.call-update) | async-done | bytes 4194320 | tf_op jit(solution)/shard_map/while/body/eval_jaxpr/all_gather | solution.py:108
  857.8 6.2 convolution_convert_fusion.9
  864.0 18.9 %reduce-scatter.35.cloned.1.call-done = bf16[256,1024]{1,0:T(8,128)(2,1)} async-done(((bf16[512,1024]{1,0:T(8,128)(2,1)}), bf16[256,1024]{1,0:T(8,128)(2,1)}) %reduce-scatter.35.cloned.1.call-update) | async-done | bytes 524304 | tf_op jit(solution)/shard_map/while/body/eval_jaxpr/reduce_scatter | solution.py:135
  889.2 21.2 %all-gather.25.cloned.1.call-done = bf16[512,1024]{1,0:T(8,128)(2,1)} async-done(((bf16[256,1024]{1,0:T(8,128)(2,1)}), bf16[512,1024]{1,0:T(8,128)(2,1)}) %all-gather.25.cloned.1.call-update) | async-done | bytes 1048592 | tf_op jit(solution)/shard_map/while/body/eval_jaxpr/all_gather | solution.py:156
  910.4 8.7 convert_reduce_fusion.6
  927.0 17.5 %reduce-scatter.37.cloned.1.call-done = bf16[256,1024]{1,0:T(8,128)(2,1)} async-done(((bf16[512,1024]{1,0:T(8,128)(2,1)}), bf16[256,1024]{1,0:T(8,128)(2,1)}) %reduce-scatter.37.cloned.1.call-update) | async-done | bytes 524304 | tf_op jit(solution)/shard_map/while/body/eval_jaxpr/reduce_scatter | solution.py:169
  949.7 10.1 select_add_fusion.11
  959.8 9.0 select_add_fusion.10
  968.9 15.9 all-gather.29.cloned.1.call-done
  984.8 22.5 %all-gather.27.cloned.1.call-done = bf16[512,1024]{1,0:T(8,128)(2,1)} async-done(((bf16[256,1024]{1,0:T(8,128)(2,1)}), bf16[512,1024]{1,0:T(8,128)(2,1)}) %all-gather.27.cloned.1.call-update) | async-done | bytes 1048592 | tf_op jit(solution)/shard_map/while/body/eval_jaxpr/all_gather | solution.py:181
  1034.1 7.4 bitcast_add_fusion.2
  1041.5 7.3 reduce-scatter.39.cloned.1.call-done
  1070.2 7.4 copy.68
  1079.6 61.4 %all-reduce = bf16[2,8,64]{1,2,0:T(8,128)(2,1)S(1)} all-reduce(bf16[2,8,64]{1,2,0:T(8,128)(2,1)S(1)} %copy.66), channel_id=8, replica_groups=mesh['dp'=16,'tensor'=2] {'dp'}, use_global_device_ids=true, to_apply=%region_26.27.clone | all-reduce | flops 1024 | bytes 4096
  1143.0 106.6 %reduce-scatter.29.cloned.1.call-done = f32[32,2]{1,0:T(8,128)} async-done(((f32[1024,2]{1,0:T(8,128)}), f32[32,2]{1,0:T(8,128)}) %reduce-scatter.29.cloned.1.call-update) | async-done | bytes 272
  1250.9 130.3 %reduce-scatter.31.cloned.1.call-done = f32[32,4]{1,0:T(8,128)} async-done(((f32[1024,4]{1,0:T(8,128)}), f32[32,4]{1,0:T(8,128)}) %reduce-scatter.31.cloned.1.call-update) | async-done | bytes 528
  1382.6 56.1 %reduce-scatter.21.cloned.1.call-done = bf16[512,64]{0,1:T(8,128)(2,1)} async-done(((bf16[512,1024]{0,1:T(8,128)(2,1)}), bf16[512,64]{0,1:T(8,128)(2,1)}) %reduce-scatter.21.cloned.1.call-update) | async-done | bytes 65552 | tf_op jit(solution)/shard_map/reduce_scatter | solution.py:247
  1440.2 67.5 %reduce-scatter.19.cloned.1.call-done = bf16[3,64,512]{2,1,0:T(8,128)(2,1)} async-done(((bf16[3,1024,512]{2,1,0:T(8,128)(2,1)}), bf16[3,64,512]{2,1,0:T(8,128)(2,1)}) %reduce-scatter.19.cloned.1.call-update) | async-done | bytes 196624 | tf_op jit(solution)/shard_map/reduce_scatter | solution.py:241
  1509.4 73.3 %reduce-scatter.23.cloned.1.call-done = bf16[64,2048]{1,0:T(8,128)(2,1)} async-done(((bf16[1024,2048]{1,0:T(8,128)(2,1)}), bf16[64,2048]{1,0:T(8,128)(2,1)}) %reduce-scatter.23.cloned.1.call-update) | async-done | bytes 262160 | tf_op jit(solution)/shard_map/reduce_scatter | solution.py:250
  1584.5 73.8 %reduce-scatter.25.cloned.1.call-done = bf16[2048,64]{0,1:T(8,128)(2,1)} async-done(((bf16[2048,1024]{0,1:T(8,128)(2,1)}), bf16[2048,64]{0,1:T(8,128)(2,1)}) %reduce-scatter.25.cloned.1.call-update) | async-done | bytes 262160 | tf_op jit(solution)/shard_map/reduce_scatter | solution.py:256
  (328 shorter events, 232.8 us)
Async XLA Ops:
  8.0 195.2 %copy-start.19 = (bf16[1,128]{1,0:T(2,128)(2,1)S(1)}, bf16[1,128]{1,0:T(2,128)(2,1)}, u32[]{:S(2)}) copy-start(bf16[1,128]{1,0:T(2,128)(2,1)} %param.19) | copy-start | bytes 772
  8.0 195.2 %copy-start.18 = (s32[2,512]{1,0:T(2,128)S(1)}, s32[2,512]{1,0:T(2,128)}, u32[]{:S(2)}) copy-start(s32[2,512]{1,0:T(2,128)} %param.14) | copy-start | bytes 12292
  9.1 8.2 collective-permute-start
  9.6 7.7 collective-permute-start.8
  17.3 7.1 collective-permute-start.1
  17.3 7.1 collective-permute-start.9
  24.4 7.2 collective-permute-start.2
  24.4 7.2 collective-permute-start.10
  31.6 7.2 collective-permute-start.3
  31.6 7.2 collective-permute-start.11
  38.8 7.2 collective-permute-start.4
  38.8 7.2 collective-permute-start.12
  46.0 7.2 collective-permute-start.5
  46.0 7.2 collective-permute-start.13
  53.2 7.1 collective-permute-start.6
  53.2 141.4 %collective-permute-start.14 = (bf16[512,64]{1,0:T(8,128)(2,1)S(1)}, bf16[512,64]{1,0:T(8,128)(2,1)S(1)}, u32[]{:S(2)}, u32[]{:S(2)}) collective-permute-start(bf16[512,64]{1,0:T(8,128)(2,1)S(1)} %collective-permute-done.13), channel_id=1, source_target_pairs={{0,30},{2,0},{4,2},{6,4},{8,6},{10,8},{12,10},{14,12},{16,14},{18,... | collective-permute-start | bytes 196616 | tf_op jit(solution)/shard_map/while/body/eval_jaxpr/ppermute | solution.py:17
  60.3 134.3 %collective-permute-start.7 = (bf16[512,64]{1,0:T(8,128)(2,1)S(1)}, bf16[512,64]{1,0:T(8,128)(2,1)S(1)}, u32[]{:S(2)}, u32[]{:S(2)}) collective-permute-start(bf16[512,64]{1,0:T(8,128)(2,1)S(1)} %collective-permute-done.6), channel_id=1, source_target_pairs={{0,2},{2,4},{4,6},{6,8},{8,10},{10,12},{12,14},{14,16},{16,18},{18... | collective-permute-start | bytes 196616 | tf_op jit(solution)/shard_map/while/body/eval_jaxpr/ppermute | solution.py:15
  203.6 22.3 %all-gather.15.cloned.1.call-start = ((), (), s32[]{:S(2)}) async-start(), calls=%async_computation.18 | async-start | bytes 1572864 | tf_op jit(solution)/shard_map/while/body/eval_jaxpr/all_gather | solution.py:110
  204.5 68.8 %all-gather.17.cloned.1.call-start = ((), (), s32[]{:S(2)}) async-start(), calls=%async_computation.19 | async-start | bytes 3342336 | tf_op jit(solution)/shard_map/while/body/eval_jaxpr/all_gather | solution.py:103
  205.3 100.3 %reduce-scatter.33.cloned.1.call-start = ((), (), s32[]{:S(2)}) async-start(), calls=%async_computation.20 | async-start | bytes 1572864 | tf_op jit(solution)/shard_map/while/body/eval_jaxpr/reduce_scatter | solution.py:122
  286.3 72.1 %all-gather.21.cloned.1.call-start = ((), (), s32[]{:S(2)}) async-start(), calls=%async_computation.22 | async-start | bytes 4456448 | tf_op jit(solution)/shard_map/while/body/eval_jaxpr/all_gather | solution.py:106
  286.9 93.4 %all-gather.19.cloned.1.call-start = ((), (), s32[]{:S(2)}) async-start(), calls=%async_computation.21 | async-start | bytes 1572864 | tf_op jit(solution)/shard_map/while/body/eval_jaxpr/all_gather | solution.py:130
  310.4 122.7 %all-gather.23.cloned.1.call-start = ((), (), s32[]{:S(2)}) async-start(), calls=%async_computation.23 | async-start | bytes 4456448 | tf_op jit(solution)/shard_map/while/body/eval_jaxpr/all_gather | solution.py:108
  311.0 147.3 %reduce-scatter.35.cloned.1.call-start = ((), (), s32[]{:S(2)}) async-start(), calls=%async_computation.24 | async-start | bytes 1572864 | tf_op jit(solution)/shard_map/while/body/eval_jaxpr/reduce_scatter | solution.py:135
  439.3 46.5 %all-gather.25.cloned.1.call-start = ((), (), s32[]{:S(2)}) async-start(), calls=%async_computation.25 | async-start | bytes 1572864 | tf_op jit(solution)/shard_map/while/body/eval_jaxpr/all_gather | solution.py:156
  464.3 55.5 %reduce-scatter.37.cloned.1.call-start = ((), (), s32[]{:S(2)}) async-start(), calls=%async_computation.26 | async-start | bytes 1572864 | tf_op jit(solution)/shard_map/while/body/eval_jaxpr/reduce_scatter | solution.py:169
  499.3 60.7 %all-gather.29.cloned.1.call-start = ((), (), s32[]{:S(2)}) async-start(), calls=%async_computation.28 | async-start | bytes 1114112 | tf_op jit(solution)/shard_map/while/body/eval_jaxpr/all_gather | solution.py:146
  499.9 82.6 %all-gather.27.cloned.1.call-start = ((), (), s32[]{:S(2)}) async-start(), calls=%async_computation.27 | async-start | bytes 1572864 | tf_op jit(solution)/shard_map/while/body/eval_jaxpr/all_gather | solution.py:181
  524.7 99.1 %reduce-scatter.39.cloned.1.call-start = ((), (), s32[]{:S(2)}) async-start(), calls=%async_computation.29 | async-start | bytes 1572864 | tf_op jit(solution)/shard_map/while/body/eval_jaxpr/reduce_scatter | solution.py:203
  626.2 24.3 %all-gather.15.cloned.1.call-start = ((), (), s32[]{:S(2)}) async-start(), calls=%async_computation.18 | async-start | bytes 1572864 | tf_op jit(solution)/shard_map/while/body/eval_jaxpr/all_gather | solution.py:110
  627.1 70.7 %all-gather.17.cloned.1.call-start = ((), (), s32[]{:S(2)}) async-start(), calls=%async_computation.19 | async-start | bytes 3342336 | tf_op jit(solution)/shard_map/while/body/eval_jaxpr/all_gather | solution.py:103
  627.7 102.3 %reduce-scatter.33.cloned.1.call-start = ((), (), s32[]{:S(2)}) async-start(), calls=%async_computation.20 | async-start | bytes 1572864 | tf_op jit(solution)/shard_map/while/body/eval_jaxpr/reduce_scatter | solution.py:122
  710.7 72.1 %all-gather.21.cloned.1.call-start = ((), (), s32[]{:S(2)}) async-start(), calls=%async_computation.22 | async-start | bytes 4456448 | tf_op jit(solution)/shard_map/while/body/eval_jaxpr/all_gather | solution.py:106
  711.3 93.4 %all-gather.19.cloned.1.call-start = ((), (), s32[]{:S(2)}) async-start(), calls=%async_computation.21 | async-start | bytes 1572864 | tf_op jit(solution)/shard_map/while/body/eval_jaxpr/all_gather | solution.py:130
  734.9 122.9 %all-gather.23.cloned.1.call-start = ((), (), s32[]{:S(2)}) async-start(), calls=%async_computation.23 | async-start | bytes 4456448 | tf_op jit(solution)/shard_map/while/body/eval_jaxpr/all_gather | solution.py:108
  735.5 147.5 %reduce-scatter.35.cloned.1.call-start = ((), (), s32[]{:S(2)}) async-start(), calls=%async_computation.24 | async-start | bytes 1572864 | tf_op jit(solution)/shard_map/while/body/eval_jaxpr/reduce_scatter | solution.py:135
  864.0 46.5 %all-gather.25.cloned.1.call-start = ((), (), s32[]{:S(2)}) async-start(), calls=%async_computation.25 | async-start | bytes 1572864 | tf_op jit(solution)/shard_map/while/body/eval_jaxpr/all_gather | solution.py:156
  889.0 55.5 %reduce-scatter.37.cloned.1.call-start = ((), (), s32[]{:S(2)}) async-start(), calls=%async_computation.26 | async-start | bytes 1572864 | tf_op jit(solution)/shard_map/while/body/eval_jaxpr/reduce_scatter | solution.py:169
  924.0 60.8 %all-gather.29.cloned.1.call-start = ((), (), s32[]{:S(2)}) async-start(), calls=%async_computation.28 | async-start | bytes 1114112 | tf_op jit(solution)/shard_map/while/body/eval_jaxpr/all_gather | solution.py:146
  924.7 82.5 %all-gather.27.cloned.1.call-start = ((), (), s32[]{:S(2)}) async-start(), calls=%async_computation.27 | async-start | bytes 1572864 | tf_op jit(solution)/shard_map/while/body/eval_jaxpr/all_gather | solution.py:181
  949.3 99.5 %reduce-scatter.39.cloned.1.call-start = ((), (), s32[]{:S(2)}) async-start(), calls=%async_computation.29 | async-start | bytes 1572864 | tf_op jit(solution)/shard_map/while/body/eval_jaxpr/reduce_scatter | solution.py:203
  1053.7 87.9 %reduce-scatter.27.cloned.1.call-start = ((), (), s32[]{:S(2)}) async-start(), calls=%async_computation.15 | async-start | bytes 557056
  1054.9 194.7 %reduce-scatter.29.cloned.1.call-start = ((), (), s32[]{:S(2)}) async-start(), calls=%async_computation.16 | async-start | bytes 540672
  1056.0 325.3 %reduce-scatter.31.cloned.1.call-start = ((), (), s32[]{:S(2)}) async-start(), calls=%async_computation.17 | async-start | bytes 540672
  1057.1 381.6 %reduce-scatter.21.cloned.1.call-start = ((), (), s32[]{:S(2)}) async-start(), calls=%async_computation.12 | async-start | bytes 1114112 | tf_op jit(solution)/shard_map/reduce_scatter | solution.py:247
  1058.6 449.2 %reduce-scatter.19.cloned.1.call-start = ((), (), s32[]{:S(2)}) async-start(), calls=%async_computation.11 | async-start | bytes 3342336 | tf_op jit(solution)/shard_map/reduce_scatter | solution.py:241
  1064.0 518.7 %reduce-scatter.23.cloned.1.call-start = ((), (), s32[]{:S(2)}) async-start(), calls=%async_computation.13 | async-start | bytes 4456448 | tf_op jit(solution)/shard_map/reduce_scatter | solution.py:250
  1070.2 588.2 %reduce-scatter.25.cloned.1.call-start = ((), (), s32[]{:S(2)}) async-start(), calls=%async_computation.14 | async-start | bytes 4456448 | tf_op jit(solution)/shard_map/reduce_scatter | solution.py:256
  (43 other events, 460.6 us)
Sparse Core Ops, SparseCore 0:
  206.6 19.2 all-gather.14
  228.1 45.1 all-gather.16
  286.4 19.1 reduce-scatter.32
  307.8 50.5 all-gather.20
  360.4 19.7 all-gather.18
  382.5 50.5 all-gather.22
  439.5 18.7 reduce-scatter.34
  464.4 21.3 all-gather.24
  499.5 20.3 reduce-scatter.36
  522.0 37.9 all-gather.28
  562.2 20.2 all-gather.26
  603.4 20.3 reduce-scatter.38
  629.2 21.2 all-gather.14
  652.6 45.1 all-gather.16
  710.9 19.1 reduce-scatter.32
  732.3 50.5 all-gather.20
  784.9 19.7 all-gather.18
  807.0 50.7 all-gather.22
  864.1 18.7 reduce-scatter.34
  889.1 21.3 all-gather.24
  924.1 20.3 reduce-scatter.36
  946.8 37.9 all-gather.28
  987.0 20.2 all-gather.26
  1028.5 20.3 reduce-scatter.38
Sparse Core Ops, SparseCore 1:
  1058.3 55.8 reduce-scatter.26
  1116.9 132.6 reduce-scatter.28
  1251.7 129.5 reduce-scatter.30
  1385.3 53.3 reduce-scatter.20
  1442.6 65.1 reduce-scatter.18
  1511.6 71.1 reduce-scatter.22
  1587.0 71.3 reduce-scatter.24
